TPU v7x, 256 devices: a whole 4x4x8 slice. The times are simulated.
256 devices in a mesh: seq: 8 (over y, core), head: 32 (over x, z).
Axes of the slice: x: 4, y: 4, z: 8, core: 2. Of those that a mesh axis runs over, the one named last changes fastest.
Arguments:
- query_rows: float32 [2, 16384, 4096], P(None, 'seq', 'head'), may hold values from -0.5 to 0.5
- key_rows: float32 [2, 16384, 4096], P(None, 'seq', 'head'), may hold values from -6 to 6
- value_rows: float32 [2, 16384, 4096], P(None, 'seq', 'head'), may hold values from -6 to 6
- cotangent: float32 [2, 16384, 4096], P(None, 'seq', 'head'), may hold values from -6 to 6
- selector: int32 [2, 32, 16384], P(None, 'head', 'seq'), may hold values from 0 to 15
- level_table: float32 [16, 4], replicated, may hold values from 0.05 to 1
- span_length: int32 [2, 8], P(None, 'seq'), may hold values from 1024 to 2048
- norm_gain: float32 [4096], P('head'), may hold values from 0.1 to 1.9
Outputs:
- attended: float32 [2, 16384, 4096], P(None, 'seq', 'head')
- state_gradient: float32 [2, 8, 128, 4096], P(None, 'seq', None, 'head')
Inputs may be any that keep to these rules, and one draw needn't show every extreme that they name: Keys at positions span_length and later of a block are padding.
All inputs are finite; a program needn't handle non-finite values.
Results may differ from a plain program's by a relative error of at most 0.0001.
Values sent between devices are 32-bit elements; how exact they have to be, the bound alone decides.
A program may use at most 128 MiB of HBM per device.

v0:
```python
import jax
import jax.numpy as jnp
from jax import lax
from jax.sharding import PartitionSpec as P

DH = 128


epsilon = 1e-06


def partner(shard, axis, stride):
    return lax.ppermute(shard, axis, [(i, i ^ 1 << stride) for i in range(lax.axis_size(axis))])


def copy_for_each(shard, axis):
    copies = jnp.broadcast_to(shard, (lax.axis_size(axis), *shard.shape))
    return lax.all_to_all(copies, axis, split_axis=0, concat_axis=0, tiled=True)


def over_copies(shard, axis):
    everything = copy_for_each(shard, axis)
    return jnp.sum(everything, axis=0)


def together(arrays, axis):
    vector, at, outs = (jnp.concatenate([a.reshape(-1) for a in arrays]), 0, [])
    subtotal = over_copies(vector, axis)
    for a in arrays:
        outs.append(subtotal[at : at + a.size].reshape(a.shape))
        at += a.size
    return tuple(outs)


def local(
    query_rows, key_rows, value_rows, cotangent, selector, level_table, span_length, norm_gain
):
    highest = lax.Precision.HIGHEST
    batch_count, token_count, local_width = query_rows.shape
    head_count = local_width // DH
    shape_four = (batch_count, token_count, head_count, DH)
    queries = query_rows.reshape(shape_four)
    values = value_rows.reshape(shape_four)
    one_hot = (selector[..., None] == jnp.arange(level_table.shape[0])[None, None, None, :]).astype(
        jnp.float32
    )
    weight = jnp.einsum("bhtc,cl->bthl", one_hot, level_table, precision=highest)
    position = jnp.arange(token_count)
    valid = (position[None, :] < span_length).astype(jnp.float32)
    live_keys = key_rows.reshape(shape_four) * valid[..., None, None]
    state = jnp.einsum("bshd,bshe->bhde", live_keys, values, precision=highest)
    causal = position[None, :] <= position[:, None]
    scores = jnp.einsum("bthd,bshd->bhts", queries, live_keys, precision=highest)
    scores = jnp.where(causal[None, None], scores, 0.0)
    combined = (
        jnp.einsum("bhts,bshe->bthe", scores, values, precision=highest) * weight[..., 0][..., None]
    )
    seq_index = lax.axis_index("seq")
    seq_count = lax.axis_size("seq")
    level_count = seq_count.bit_length() - 1
    block_sum = state
    for level_bit in range(level_count):
        received = partner(block_sum, "seq", level_bit)
        reads_bucket = (seq_index >> level_bit & 1).astype(jnp.float32)
        reads = jnp.einsum("bthd,bhde->bthe", queries, received, precision=highest)
        combined = combined + reads * (weight[..., level_bit + 1] * reads_bucket)[..., None]
        block_sum = block_sum + received
    combined = combined.reshape(batch_count, token_count, local_width)
    scaled = cotangent * norm_gain
    square_sum, inner_sum = together(
        (jnp.sum(combined * combined, axis=2), jnp.sum(scaled * combined, axis=2)), "head"
    )
    full_width = local_width * lax.axis_size("head")
    inverse = lax.rsqrt(square_sum / full_width + epsilon)
    attended = combined * inverse[..., None] * norm_gain
    combined_grad = (
        scaled * inverse[..., None]
        - combined * (inverse * inverse * inverse * inner_sum / full_width)[..., None]
    )
    grad_four = combined_grad.reshape(shape_four)
    level_grads = []
    for level_bit in range(level_count):
        reads_bucket = (seq_index >> level_bit & 1).astype(jnp.float32)
        weighted = queries * (weight[..., level_bit + 1] * reads_bucket)[..., None]
        level_grads.append(jnp.einsum("bthd,bthe->bhde", weighted, grad_four, precision=highest))
    stacked = jnp.stack(level_grads, axis=0)
    pending = stacked
    state_grad = jnp.zeros(state.shape, jnp.float32)
    for level_bit in range(level_count):
        received = partner(pending, "seq", level_bit)
        lower_half = (1 - (seq_index >> level_bit & 1)).astype(jnp.float32)
        state_grad = state_grad + lower_half * received[0]
        pending = pending[1:] + received[1:]
    state_gradient = state_grad.transpose(0, 2, 1, 3).reshape(batch_count, 1, DH, head_count * DH)
    return (attended, state_gradient)


def solution(mesh):
    return jax.shard_map(
        local,
        mesh=mesh,
        in_specs=(
            P(None, "seq", "head"),
            P(None, "seq", "head"),
            P(None, "seq", "head"),
            P(None, "seq", "head"),
            P(None, "head", "seq"),
            P(),
            P(None, "seq"),
            P("head"),
        ),
        out_specs=(P(None, "seq", "head"), P(None, "seq", None, "head")),
        check_vma=False,
    )
```

profile of v0, /device:TPU:1, one launch (start us, length us, event | category | flops | bytes accessed | tf_op | source)
XLA Modules:
  0.0 166.3 jit_solution(11760655495369557145)
XLA Ops:
  2.2 5.6 %fusion.22 = f32[2,1,128,128]{3,2,0,1:T(8,128)S(1)} fusion(f32[2,2048,128]{2,1,0:T(8,128)S(1)} %copy-done, f32[2,2048,128]{2,1,0:T(8,128)} %param.9, f32[2,2048]{1,0:T(2,128)S(1)} %compare_convert_fusion), kind=kOutput, calls=%fused_computation.32 | convolution fusion | flops 805830656 | bytes 4341760 | tf_op jit(solution)/shard_map/bshd,bshe->bhde/dot_general | solution.py:51
  7.9 3.3 %collective-permute-start = (f32[2,1,128,128]{3,2,0,1:T(8,128)S(1)}, f32[2,1,128,128]{3,2,0,1:T(8,128)S(1)}, u32[]{:S(2)}, u32[]{:S(2)}) collective-permute-start(f32[2,1,128,128]{3,2,0,1:T(8,128)S(1)} %fusion.22), channel_id=1, source_target_pairs={{0,32},{32,0},{64,96},{96,64},{128,160},{160,128},{192,224},{224,1... | collective-permute-start | bytes 393224 | tf_op jit(solution)/shard_map/ppermute | solution.py:13
  11.2 4.2 %iota_compare_fusion = pred[2048,2048]{0,1:T(8,128)(4,1)} fusion(), kind=kLoop, calls=%fused_computation.3 | loop fusion | flops 4194304 | bytes 4194304 | tf_op jit(solution)/shard_map/le | solution.py:52
  15.4 31.8 %fusion.20 = f32[2,2048,2048]{2,1,0:T(8,128)} fusion(f32[2,2048,128]{2,1,0:T(8,128)} %param.8, f32[2,2048,128]{2,1,0:T(8,128)} %param.9, f32[2,2048]{1,0:T(2,128)S(1)} %compare_convert_fusion), kind=kOutput, calls=%fused_computation.30 | convolution fusion | flops 12885426176 | bytes 37765120 | tf_op jit(solution)/shard_map/bthd,bshd->bhts/dot_general | solution.py:53
  47.6 27.4 %fusion.4 = f32[2,1,128,2048]{3,2,0,1:T(8,128)} fusion(f32[2,2048,128]{2,1,0:T(8,128)S(1)} %copy-done, f32[2,2048,2048]{2,1,0:T(8,128)} %fusion.20, pred[2048,2048]{0,1:T(8,128)(4,1)S(1)} %copy-done.3, f32[2,2048]{1,0:T(2,128)S(1)} %get-tuple-element.22), kind=kOutput, calls=%fused_computation.9 | convolution fusion | flops 12893814784 | bytes 41959424 | tf_op jit(solution)/shard_map/bhts,bshe->bthe/dot_general | solution.py:56
  75.1 3.0 %copy.44 = f32[2,2048,128]{1,2,0:T(8,128)} copy(f32[2,2048,128]{2,1,0:T(8,128)} %param.11) | data formatting | bytes 4194304 | tf_op args[3]
  78.2 2.0 %collective-permute-done.1 = f32[2,1,128,128]{3,2,0,1:T(8,128)S(1)} collective-permute-done((f32[2,1,128,128]{3,2,0,1:T(8,128)S(1)}, f32[2,1,128,128]{3,2,0,1:T(8,128)S(1)}, u32[]{:S(2)}, u32[]{:S(2)}) %collective-permute-start.1) | collective-permute-done | bytes 131104 | tf_op jit(solution)/shard_map/ppermute | solution.py:13
  80.2 1.5 collective-permute-start.2
  81.7 2.0 %fusion.10 = f32[2,1,128,2048]{3,2,0,1:T(8,128)S(1)} fusion(f32[2,2048,128]{2,1,0:T(8,128)S(1)} %copy-done.2, f32[2,2048]{1,0:T(2,128)S(1)} %get-tuple-element.20, f32[2,1,128,128]{3,2,0,1:T(8,128)S(1)} %collective-permute-done.1), kind=kOutput, calls=%fused_computation.15 | convolution fusion | flops 805830656 | bytes 4341760 | tf_op jit(solution)/shard_map/bthd,bhde->bthe/dot_general | solution.py:65
  83.7 2.5 %collective-permute-done.2 = f32[2,1,128,128]{3,2,0,1:T(8,128)S(1)} collective-permute-done((f32[2,1,128,128]{3,2,0,1:T(8,128)S(1)}, f32[2,1,128,128]{3,2,0,1:T(8,128)S(1)}, u32[]{:S(2)}, u32[]{:S(2)}) %collective-permute-start.2) | collective-permute-done | bytes 131104 | tf_op jit(solution)/shard_map/ppermute | solution.py:13
  86.2 2.0 %fusion.11 = f32[2,1,128,2048]{3,2,0,1:T(8,128)S(1)} fusion(f32[2,2048,128]{2,1,0:T(8,128)S(1)} %copy-done.2, f32[2,2048]{1,0:T(2,128)S(1)} %get-tuple-element.19, f32[2,1,128,128]{3,2,0,1:T(8,128)S(1)} %collective-permute-done.2), kind=kOutput, calls=%fused_computation.16 | convolution fusion | flops 805830656 | bytes 4341760 | tf_op jit(solution)/shard_map/bthd,bhde->bthe/dot_general | solution.py:65
  88.4 4.1 %multiply_reduce_fusion.1 = (f32[2,2048]{1,0:T(2,128)S(1)}, f32[2,2048]{1,0:T(2,128)S(1)}, f32[2,2048,128]{1,2,0:T(8,128)}) fusion(f32[2,2048,128]{1,2,0:T(8,128)S(1)} %copy-done.4, f32[128]{0:T(128)S(1)} %copy-done.7, f32[2,1,128,2048]{3,2,0,1:T(8,128)S(1)} %fusion.11, f32[2,1,128,2048]{3,2,0,1:T(8,128)S(1)} %fusion.10, ...), kind=kOutput, calls=%fused_computation.27 | convolution fusion | flops 810016768 | bytes 12763648 | tf_op jit(solution)/shard_map/bthd,bhde->bthe/dot_general | solution.py:65
  92.6 0.9 broadcast_in_dim.16
  93.5 33.6 %all_to_all.6 = f32[32,1,8192]{2,1,0:T(1,128)S(1)} all-to-all(f32[32,1,8192]{2,1,0:T(1,128)S(1)} %broadcast_in_dim.16), channel_id=1, replica_groups=mesh['seq'=8,'head'=32] {'head'}, dimensions={0} | all-to-all | bytes 2097152 | tf_op jit(solution)/shard_map/all_to_all | solution.py:18
  127.9 4.3 %multiply_subtract_fusion = (f32[2,2048,128]{1,2,0:T(8,128)S(1)}, f32[2,2048,128]{1,2,0:T(8,128)}) fusion(f32[2,2048,128]{1,2,0:T(8,128)} %get-tuple-element.18, f32[2,2048,128]{1,2,0:T(8,128)} %copy.44, f32[2,2048]{1,0:T(2,128)S(1)} %fusion.47, f32[2,2048]{1,0:T(2,128)S(1)} %rsqrt.7, f32[128]{0:T(128)S(1)} %copy-done.7), kind=kLoop, calls=%fused_computation.22 | loop fusion | flops 3145728 | bytes 8421888 | tf_op jit(solution)/shard_map/sub | solution.py:77
  132.2 4.3 %fusion.25 = f32[1,2,1,128,128]{4,3,1,2,0:T(8,128)S(1)} fusion(f32[2,2048,128]{1,2,0:T(8,128)S(1)} %get-tuple-element.10, f32[2,2048,128]{2,1,0:T(8,128)S(1)} %copy-done.2, f32[2,2048]{1,0:T(2,128)S(1)} %get-tuple-element.21), kind=kOutput, calls=%fused_computation.33 | convolution fusion | flops 805830656 | bytes 4341760 | tf_op jit(solution)/shard_map/bthd,bthe->bhde/dot_general | solution.py:85
  136.5 4.3 %fusion.28 = f32[1,2,1,128,128]{4,3,1,2,0:T(8,128)S(1)} fusion(f32[2,2048,128]{1,2,0:T(8,128)S(1)} %get-tuple-element.10, f32[2,2048,128]{2,1,0:T(8,128)S(1)} %copy-done.2, f32[2,2048]{1,0:T(2,128)S(1)} %get-tuple-element.20), kind=kOutput, calls=%fused_computation.34 | convolution fusion | flops 805830656 | bytes 4341760 | tf_op jit(solution)/shard_map/bthd,bthe->bhde/dot_general | solution.py:85
  140.9 4.3 %fusion.31 = f32[1,2,1,128,128]{4,3,1,2,0:T(8,128)S(1)} fusion(f32[2,2048,128]{1,2,0:T(8,128)S(1)} %get-tuple-element.10, f32[2,2048,128]{2,1,0:T(8,128)S(1)} %copy-done.2, f32[2,2048]{1,0:T(2,128)S(1)} %get-tuple-element.19), kind=kOutput, calls=%fused_computation.35 | convolution fusion | flops 805830656 | bytes 4341760 | tf_op jit(solution)/shard_map/bthd,bthe->bhde/dot_general | solution.py:85
  145.2 5.3 %collective-permute-start.3 = (f32[3,2,1,128,128]{4,3,1,2,0:T(8,128)S(1)}, f32[3,2,1,128,128]{4,3,1,2,0:T(8,128)S(1)}, u32[]{:S(2)}, u32[]{:S(2)}) collective-permute-start(f32[3,2,1,128,128]{4,3,1,2,0:T(8,128)S(1)} %pad_maximum_fusion), channel_id=1, source_target_pairs={{0,32},{32,0},{64,96},{96,64},{128,160},{160,128},{192,224},{224,1... | collective-permute-start | bytes 1179656 | tf_op jit(solution)/shard_map/ppermute | solution.py:13
  150.5 1.3 collective-permute-done.3
  151.9 1.5 collective-permute-start.4
  153.4 6.1 %collective-permute-done.4 = f32[2,2,1,128,128]{4,3,1,2,0:T(8,128)S(1)} collective-permute-done((f32[2,2,1,128,128]{4,3,1,2,0:T(8,128)S(1)}, f32[2,2,1,128,128]{4,3,1,2,0:T(8,128)S(1)}, u32[]{:S(2)}, u32[]{:S(2)}) %collective-permute-start.4) | collective-permute-done | bytes 262176 | tf_op jit(solution)/shard_map/ppermute | solution.py:13
  159.5 3.0 %collective-permute-start.5 = (f32[1,2,1,128,128]{4,3,1,2,0:T(8,128)S(1)}, f32[1,2,1,128,128]{4,3,1,2,0:T(8,128)S(1)}, u32[]{:S(2)}, u32[]{:S(2)}) collective-permute-start(f32[1,2,1,128,128]{4,3,1,2,0:T(8,128)S(1)} %slice_add_fusion.1), channel_id=1, source_target_pairs={{0,128},{32,160},{64,192},{96,224},{128,0},{160,32},{192,64},{224,... | collective-permute-start | bytes 393224 | tf_op jit(solution)/shard_map/ppermute | solution.py:13
  162.6 3.0 %copy.52 = f32[2,2048,128]{2,1,0:T(8,128)} copy(f32[2,2048,128]{1,2,0:T(8,128)} %get-tuple-element.11) | data formatting | bytes 4194304
  (41 shorter events, 3.8 us)
Async XLA Ops:
  0.6 1.6 copy-start
  7.9 67.1 %collective-permute-start = (f32[2,1,128,128]{3,2,0,1:T(8,128)S(1)}, f32[2,1,128,128]{3,2,0,1:T(8,128)S(1)}, u32[]{:S(2)}, u32[]{:S(2)}) collective-permute-start(f32[2,1,128,128]{3,2,0,1:T(8,128)S(1)} %fusion.22), channel_id=1, source_target_pairs={{0,32},{32,0},{64,96},{96,64},{128,160},{160,128},{192,224},{224,1... | collective-permute-start | bytes 393224 | tf_op jit(solution)/shard_map/ppermute | solution.py:13
  11.2 4.2 %copy-start.6 = (s32[2,1,2048]{2,1,0:T(1,128)S(1)}, s32[2,1,2048]{2,1,0:T(1,128)}, u32[]{:S(2)}) copy-start(s32[2,1,2048]{2,1,0:T(1,128)} %param.12) | copy-start | bytes 49156
  15.4 31.9 %copy-start.8 = (f32[16,4]{0,1:T(4,128)S(1)}, f32[16,4]{0,1:T(4,128)}, u32[]{:S(2)}) copy-start(f32[16,4]{0,1:T(4,128)} %param.13) | copy-start | bytes 772
  15.4 32.2 %copy-start.3 = (pred[2048,2048]{0,1:T(8,128)(4,1)S(1)}, pred[2048,2048]{0,1:T(8,128)(4,1)}, u32[]{:S(2)}) copy-start(pred[2048,2048]{0,1:T(8,128)(4,1)} %iota_compare_fusion) | copy-start | bytes 12582916
  75.0 5.2 %collective-permute-start.1 = (f32[2,1,128,128]{3,2,0,1:T(8,128)S(1)}, f32[2,1,128,128]{3,2,0,1:T(8,128)S(1)}, u32[]{:S(2)}, u32[]{:S(2)}) collective-permute-start(f32[2,1,128,128]{3,2,0,1:T(8,128)S(1)} %add.60), channel_id=1, source_target_pairs={{0,64},{32,96},{64,0},{96,32},{128,192},{160,224},{192,128},{224,1... | collective-permute-start | bytes 393224 | tf_op jit(solution)/shard_map/ppermute | solution.py:13
  75.1 6.6 %copy-start.2 = (f32[2,2048,128]{2,1,0:T(8,128)S(1)}, f32[2,2048,128]{2,1,0:T(8,128)}, u32[]{:S(2)}) copy-start(f32[2,2048,128]{2,1,0:T(8,128)} %param.8) | copy-start | bytes 6291460
  80.2 6.0 %collective-permute-start.2 = (f32[2,1,128,128]{3,2,0,1:T(8,128)S(1)}, f32[2,1,128,128]{3,2,0,1:T(8,128)S(1)}, u32[]{:S(2)}, u32[]{:S(2)}) collective-permute-start(f32[2,1,128,128]{3,2,0,1:T(8,128)S(1)} %add.62), channel_id=1, source_target_pairs={{0,128},{32,160},{64,192},{96,224},{128,0},{160,32},{192,64},{224,... | collective-permute-start | bytes 393224 | tf_op jit(solution)/shard_map/ppermute | solution.py:13
  86.2 2.0 %copy-start.4 = (f32[2,2048,128]{1,2,0:T(8,128)S(1)}, f32[2,2048,128]{1,2,0:T(8,128)}, u32[]{:S(2)}) copy-start(f32[2,2048,128]{1,2,0:T(8,128)} %copy.44) | copy-start | bytes 6291460
  86.2 2.2 %copy-start.5 = (f32[2,1,128,2048]{3,2,0,1:T(8,128)S(1)}, f32[2,1,128,2048]{3,2,0,1:T(8,128)}, u32[]{:S(2)}) copy-start(f32[2,1,128,2048]{3,2,0,1:T(8,128)} %fusion.4) | copy-start | bytes 6291460
  86.2 2.2 %copy-start.7 = (f32[128]{0:T(128)S(1)}, f32[128]{0:T(128)}, u32[]{:S(2)}) copy-start(f32[128]{0:T(128)} %param.15) | copy-start | bytes 1540
  145.2 6.7 %collective-permute-start.3 = (f32[3,2,1,128,128]{4,3,1,2,0:T(8,128)S(1)}, f32[3,2,1,128,128]{4,3,1,2,0:T(8,128)S(1)}, u32[]{:S(2)}, u32[]{:S(2)}) collective-permute-start(f32[3,2,1,128,128]{4,3,1,2,0:T(8,128)S(1)} %pad_maximum_fusion), channel_id=1, source_target_pairs={{0,32},{32,0},{64,96},{96,64},{128,160},{160,128},{192,224},{224,1... | collective-permute-start | bytes 1179656 | tf_op jit(solution)/shard_map/ppermute | solution.py:13
  151.9 7.6 %collective-permute-start.4 = (f32[2,2,1,128,128]{4,3,1,2,0:T(8,128)S(1)}, f32[2,2,1,128,128]{4,3,1,2,0:T(8,128)S(1)}, u32[]{:S(2)}, u32[]{:S(2)}) collective-permute-start(f32[2,2,1,128,128]{4,3,1,2,0:T(8,128)S(1)} %slice_add_fusion), channel_id=1, source_target_pairs={{0,64},{32,96},{64,0},{96,32},{128,192},{160,224},{192,128},{224,1... | collective-permute-start | bytes 786440 | tf_op jit(solution)/shard_map/ppermute | solution.py:13
  159.5 6.1 %collective-permute-start.5 = (f32[1,2,1,128,128]{4,3,1,2,0:T(8,128)S(1)}, f32[1,2,1,128,128]{4,3,1,2,0:T(8,128)S(1)}, u32[]{:S(2)}, u32[]{:S(2)}) collective-permute-start(f32[1,2,1,128,128]{4,3,1,2,0:T(8,128)S(1)} %slice_add_fusion.1), channel_id=1, source_target_pairs={{0,128},{32,160},{64,192},{96,224},{128,0},{160,32},{192,64},{224,... | collective-permute-start | bytes 393224 | tf_op jit(solution)/shard_map/ppermute | solution.py:13
  162.6 3.7 %copy-start.1 = (f32[2,2048,128]{2,1,0:T(8,128)S(1)}, f32[2,2048,128]{2,1,0:T(8,128)}, u32[]{:S(2)}) copy-start(f32[2,2048,128]{2,1,0:T(8,128)} %param.10) | copy-start | bytes 6291460
where the time goes:
time: 167 us; the launch traced here: 166 us
  matrix products  86 us (51%)
  blocking collectives  33.6 us (20%)
  starting transfers between devices  14.7 us (9%)
  waiting for transfers between devices  12 us (7%)
  other arithmetic  11 us (7%)
  local copies, waits for them, and re-layouts  8.07 us (5%)
    all_to_all x1, blocking collectives, copy_for_each(): return lax.all_to_all(copies, axis, split_axis=0, concat_axis=0, tiled=True)  33.6 us
    dot_general x1, matrix products, local(): jnp.einsum('bthd,bshd->bhts', queries, live_keys, precision=highest)  31.8 us
    dot_general x1, matrix products, local(): jnp.einsum('bhts,bshe->bthe', scores, values, precision=highest)  27.4 us
    ppermute x6, starting transfers between devices, partner(): lax.ppermute(shard, axis, [(i, i ^ 1 << stride) for i in range(lax.axis_s...  14.7 us
    dot_general x3, matrix products, local(): jnp.einsum('bthd,bthe->bhde', weighted, grad_four, precision=highest)  13 us
    ppermute x6, waiting for transfers between devices, partner(): lax.ppermute(shard, axis, [(i, i ^ 1 << stride) for i in range(lax.axis_s...  12 us
    dot_general x3, matrix products, local(): reads = jnp.einsum('bthd,bhde->bthe', queries, received, precision=highest)  8.03 us
    unnamed x25, local copies, waits for them, and re-layouts  7.11 us
  transfers between devices with their start and end apart: 6, of which 4 were waited for; matrix products, arithmetic and copies ran while one was open for 43% of the time, Pallas kernels for 0%

commit v1 on v0

v1 whole, which is shorter than its diff:
```python
import functools

import jax
import jax.numpy as jnp
from jax import lax
from jax.experimental import pallas as pl
from jax.experimental.pallas import tpu as pltpu
from jax.sharding import PartitionSpec as P

DH = 128
CHUNK = 256
WIDE = 512
EPS = 1e-06
F32 = jnp.float32
BF16 = jnp.bfloat16


def split(x):
    high = x.astype(BF16)
    return high, (x - high.astype(F32)).astype(BF16)


def mm(a, b):
    return jnp.dot(a, b, preferred_element_type=F32)


def mm_nt(a, b):
    return lax.dot_general(a, b, (((1,), (1,)), ((), ())), preferred_element_type=F32)


def remote(src, dst, send_sem, recv_sem, device):
    return pltpu.make_async_remote_copy(
        src_ref=src,
        dst_ref=dst,
        send_sem=send_sem,
        recv_sem=recv_sem,
        device_id=device,
        device_id_type=pl.DeviceIdType.MESH,
    )


def kernel(
    n_head, tokens,
    q_hbm, k_hbm, v_hbm, c_hbm, sel_ref, tab_ref, span_ref, gain_ref,
    att_hbm, sg_ref,
    qb, kb, vb, cb, kh, kl, vt, pp, wrow, wq, comb, sc, gacc, attb,
    st, b0, pair, b12, quad, lb, sums, sums_in, coef, gr, t1, t1c, r12, r12_in, r3, total, t4,
    load_sem, out_sem, send_sem, recv_sem, h_send, h_recv,
):
    n_chunks = tokens // CHUNK
    per_batch = n_head // 2
    seq = lax.axis_index("seq")
    head = lax.axis_index("head")
    core = lax.rem(seq, 2)
    other = 1 - core
    chip = lax.div(seq, 2)
    y_a = chip + 1 - 2 * lax.rem(chip, 2)
    y_b = 3 - chip
    mate = seq + 1 - 2 * core
    near = 2 * y_a + core
    far = 2 * y_b + core

    loads = {}
    for b in range(2):
        for i, (name, src, dst) in enumerate((("k", k_hbm, kb), ("v", v_hbm, vb))):
            loads[name, b] = pltpu.make_async_copy(src.at[b], dst.at[b], load_sem.at[i, b])
            loads[name, b].start()
    for b in range(2):
        for i, (name, src, dst) in enumerate((("q", q_hbm, qb), ("c", c_hbm, cb))):
            loads[name, b] = pltpu.make_async_copy(src.at[b], dst.at[b], load_sem.at[2 + i, b])
            loads[name, b].start()

    barrier = pltpu.get_barrier_semaphore()
    for peer in (mate, near, far):
        pl.semaphore_signal(barrier, 1, device_id={"seq": peer, "head": head}, device_id_type=pl.DeviceIdType.MESH)

    @pl.loop(1, n_head)
    def _(r):
        peer = lax.rem(head + r, n_head)
        pl.semaphore_signal(barrier, 1, device_id={"seq": seq, "head": peer}, device_id_type=pl.DeviceIdType.MESH)

    selector = [sel_ref[b] for b in range(2)]
    for level in range(4):
        on = 1 if level == 0 else lax.rem(lax.div(seq, 2 ** (level - 1)), 2)
        for b in range(2):
            row = jnp.zeros((1, tokens), F32)
            for choice in range(16):
                row = jnp.where(selector[b] == choice, tab_ref[choice, level], row)
            if level > 0:
                row = jnp.where(on == 1, row, 0.0)
            wrow[level * 2 + b] = row

    for b in range(2):
        loads["k", b].wait()
        loads["v", b].wait()
        span = span_ref[b, 0]

        def state_step(n, acc, b=b, span=span):
            rows = pl.ds(pl.multiple_of(n * CHUNK, CHUNK), CHUNK)
            position = n * CHUNK + lax.broadcasted_iota(jnp.int32, (CHUNK, DH), 0)
            k_hi, k_lo = split(jnp.where(position < span, kb[b, rows, :], 0.0))
            kh[b, rows, :] = k_hi
            kl[b, rows, :] = k_lo
            v_hi, v_lo = split(vb[b, rows, :].T)
            v_two = jnp.concatenate([v_hi, v_lo], axis=0)
            vt[b, n] = v_two
            p_hi, p_lo = split(acc)
            pp[b, n] = jnp.concatenate([p_hi, p_lo], axis=0)
            out = mm(v_two, jnp.concatenate([k_hi, k_lo], axis=1))
            return acc + (out[:DH, :DH] + (out[:DH, DH:] + out[DH:, :DH]))

        st[b] = lax.fori_loop(0, n_chunks, state_step, jnp.zeros((DH, DH), F32))

    pl.semaphore_wait(barrier, n_head - 1 + 3)

    def to(peer):
        return {"seq": peer, "head": head}

    s1 = remote(st, b0, send_sem.at[0], recv_sem.at[0], to(mate))
    s1.start()

    def local_chunk(b, n):
        rows = pl.ds(pl.multiple_of(n * CHUNK, CHUNK), CHUNK)
        q_t = qb[b, rows, :].T
        q_hi, q_lo = split(q_t)
        k_hi, k_lo = kh[b, rows, :], kl[b, rows, :]
        scores = mm(
            jnp.concatenate([k_hi, k_hi, k_lo], axis=1), jnp.concatenate([q_hi, q_lo, q_hi], axis=0)
        )
        key_at = lax.broadcasted_iota(jnp.int32, (CHUNK, CHUNK), 0)
        query_at = lax.broadcasted_iota(jnp.int32, (CHUNK, CHUNK), 1)
        s_hi, s_lo = split(jnp.where(key_at <= query_at, scores, 0.0))
        v_two, p_two = vt[b, n], pp[b, n]
        out = mm(
            jnp.concatenate([v_two, v_two, p_two, p_two], axis=1),
            jnp.concatenate([s_hi, s_lo, q_hi, q_lo], axis=0),
        )
        comb[b, n] = (out[:DH] + out[DH:]) * wrow[b, :, rows]
        for level in range(3):
            w_hi, w_lo = split(q_t * wrow[2 * (level + 1) + b, :, rows])
            wq[b, level * DH : (level + 1) * DH, rows] = w_hi
            wq[b, (3 + level) * DH : (4 + level) * DH, rows] = w_lo
        sc[b, n] = (cb[b, rows, :] * gain_ref[...]).T

    def local_chunks(b, low, high):
        @pl.loop(low, high)
        def _(n):
            local_chunk(b, n)

    half = n_chunks // 2
    loads["q", 0].wait()
    loads["c", 0].wait()
    local_chunks(0, 0, half)

    s1.wait_recv()
    pair[...] = st[core] + b0[core]
    s2 = remote(pair, b12.at[core, 0], send_sem.at[1], recv_sem.at[1], to(near))
    s2.start()
    local_chunks(0, half, n_chunks)
    s2.wait_recv()
    quad[...] = pair[...] + b12[core, 0]
    s3 = remote(quad, b12.at[core, 1], send_sem.at[2], recv_sem.at[2], to(far))
    s3.start()
    s4a = remote(b12.at[core, 0], b12.at[core, 0], send_sem.at[3], recv_sem.at[3], to(mate))
    s4a.start()
    loads["q", 1].wait()
    loads["c", 1].wait()
    local_chunks(1, 0, half)
    s3.wait_recv()
    s4b = remote(b12.at[core, 1], b12.at[core, 1], send_sem.at[4], recv_sem.at[4], to(mate))
    s4b.start()
    local_chunks(1, half, n_chunks)

    def head_copy(peer):
        return remote(
            sums.at[peer], sums_in.at[head], h_send.at[0], h_recv.at[0], {"seq": seq, "head": peer}
        )

    def reads(b):
        halves = [split(b0[b]), split(b12[b, 0]), split(b12[b, 1])]
        high = jnp.concatenate([h[0] for h in halves], axis=1)
        low = jnp.concatenate([h[1] for h in halves], axis=1)
        lb[b, :DH] = jnp.concatenate([high, high], axis=1)
        lb[b, DH:] = jnp.concatenate([low, low], axis=1)

        @pl.loop(0, n_chunks)
        def _(n):
            rows = pl.ds(pl.multiple_of(n * CHUNK, CHUNK), CHUNK)
            out = mm(lb[b], wq[b, :, rows])
            mixed = comb[b, n] + (out[:DH] + out[DH:])
            comb[b, n] = mixed
            square = jnp.sum(mixed * mixed, axis=0, keepdims=True)
            inner = jnp.sum(sc[b, n] * mixed, axis=0, keepdims=True)
            for part in range(2):
                owner = b * per_batch + 2 * n + part
                lanes = slice(part * DH, (part + 1) * DH)
                sums[owner, 0:1, :] = square[:, lanes]
                sums[owner, 1:2, :] = inner[:, lanes]

        @pl.loop(0, per_batch)
        def _(j):
            peer = b * per_batch + j

            @pl.when(peer != head)
            def _():
                head_copy(peer).start()

    reads(core)
    s4a.wait_recv()
    s4b.wait_recv()
    reads(other)

    def all_but_one(buffer, sem):
        window = buffer.at[pl.ds(0, n_head - 1)]
        pltpu.make_async_copy(window, window, sem).wait()

    sums_in[head] = sums[head]
    all_but_one(sums_in, h_recv.at[0])
    whole = jnp.sum(sums_in[...], axis=0)
    inverse = lax.rsqrt(whole[0:1] / (n_head * DH) + EPS)
    coef[head, 0:1, :] = inverse
    coef[head, 1:2, :] = inverse * inverse * inverse * whole[1:2] / (n_head * DH)

    @pl.loop(1, n_head)
    def _(r):
        peer = lax.rem(head + r, n_head)
        remote(
            coef.at[head], coef.at[head], h_send.at[1], h_recv.at[1], {"seq": seq, "head": peer}
        ).start()

    all_but_one(coef, h_recv.at[1])

    wide_chunks = tokens // WIDE

    def row_of(b, n, which, width):
        first = b * per_batch + n * (width // DH)
        return jnp.concatenate(
            [coef[first + i, which : which + 1, :] for i in range(width // DH)], axis=1
        )

    def level_grads(b):
        gacc[...] = jnp.zeros_like(gacc)

        @pl.loop(0, wide_chunks)
        def _(n):
            rows = pl.ds(pl.multiple_of(n * WIDE, WIDE), WIDE)
            pieces = WIDE // CHUNK
            scaled = jnp.concatenate([sc[b, n * pieces + i] for i in range(pieces)], axis=1)
            mixed = jnp.concatenate([comb[b, n * pieces + i] for i in range(pieces)], axis=1)
            grad = scaled * row_of(b, n, 0, WIDE) - mixed * row_of(b, n, 1, WIDE)
            g_hi, g_lo = split(grad)
            gacc[...] += mm_nt(wq[b, :, rows], jnp.concatenate([g_hi, g_lo], axis=0))

        for level in range(3):
            top = slice(level * DH, (level + 1) * DH)
            bottom = slice((3 + level) * DH, (4 + level) * DH)
            gr[b, level] = gacc[top, :DH] + (gacc[top, DH:] + gacc[bottom, :DH])

    def attended(b):
        @pl.loop(0, n_chunks)
        def _(n):
            rows = pl.ds(pl.multiple_of(n * CHUNK, CHUNK), CHUNK)
            attb[b, rows, :] = (comb[b, n] * row_of(b, n, 0, CHUNK)).T * gain_ref[...]

        pltpu.make_async_copy(attb.at[b], att_hbm.at[b], out_sem.at[b]).start()

    level_grads(core)
    g1 = remote(gr.at[core], t1, send_sem.at[5], recv_sem.at[5], to(mate))
    g1.start()
    level_grads(other)
    g1c = remote(gr.at[other, 0], t1c, send_sem.at[6], recv_sem.at[6], to(mate))
    g1c.start()
    g1.wait_recv()
    r12[0] = gr[other, 1] + t1[1]
    r12[1] = gr[other, 2] + t1[2]
    g2a = remote(r12.at[0], r12_in.at[0], send_sem.at[7], recv_sem.at[7], to(near))
    g2b = remote(r12.at[1], r12_in.at[1], send_sem.at[8], recv_sem.at[8], to(far))
    g2b.start()
    g2a.start()
    attended(0)
    g2b.wait_recv()
    g3 = remote(r12_in.at[1], r3, send_sem.at[9], recv_sem.at[9], to(near))
    g3.start()
    attended(1)
    g2a.wait_recv()
    g3.wait_recv()
    total[...] = r12_in[0] + r12_in[1] + r3[...]
    g4 = remote(total, t4, send_sem.at[10], recv_sem.at[10], to(mate))
    g4.start()
    sg_ref[other, 0] = total[...] + t1[0]
    g1c.wait_recv()
    g4.wait_recv()
    sg_ref[core, 0] = t4[...] + t1c[...]

    for copy in (s1, s2, s3, s4a, s4b, g1, g1c, g2a, g2b, g3, g4):
        copy.wait_send()
    all_but_one(sums, h_send.at[0])
    all_but_one(coef, h_send.at[1])
    for b in range(2):
        pltpu.make_async_copy(attb.at[b], att_hbm.at[b], out_sem.at[b]).wait()


def solution(mesh):
    n_head = mesh.shape["head"]

    def local(
        query_rows, key_rows, value_rows, cotangent, selector, level_table, span_length, norm_gain
    ):
        batch, tokens, _ = query_rows.shape
        n_chunks = tokens // CHUNK
        square = (DH, DH)
        whole = (batch, tokens, DH)
        scratch = [pltpu.VMEM(whole, F32) for _ in range(4)]
        scratch += [
            pltpu.VMEM(whole, BF16),
            pltpu.VMEM(whole, BF16),
            pltpu.VMEM((batch, n_chunks, 2 * DH, CHUNK), BF16),
            pltpu.VMEM((batch, n_chunks, 2 * DH, DH), BF16),
            pltpu.VMEM((4 * batch, 1, tokens), F32),
            pltpu.VMEM((batch, 6 * DH, tokens), BF16),
            pltpu.VMEM((batch, n_chunks, DH, CHUNK), F32),
            pltpu.VMEM((batch, n_chunks, DH, CHUNK), F32),
            pltpu.VMEM((6 * DH, 2 * DH), F32),
            pltpu.VMEM(whole, F32),
            pltpu.VMEM((batch, *square), F32),
            pltpu.VMEM((batch, *square), F32),
            pltpu.VMEM(square, F32),
            pltpu.VMEM((batch, 2, *square), F32),
            pltpu.VMEM(square, F32),
            pltpu.VMEM((batch, 2 * DH, 6 * DH), BF16),
            pltpu.VMEM((n_head, 2, DH), F32),
            pltpu.VMEM((n_head, 2, DH), F32),
            pltpu.VMEM((n_head, 2, DH), F32),
            pltpu.VMEM((batch, 3, *square), F32),
            pltpu.VMEM((3, *square), F32),
            pltpu.VMEM(square, F32),
            pltpu.VMEM((2, *square), F32),
            pltpu.VMEM((2, *square), F32),
            pltpu.VMEM(square, F32),
            pltpu.VMEM(square, F32),
            pltpu.VMEM(square, F32),
            pltpu.SemaphoreType.DMA((4, 2)),
            pltpu.SemaphoreType.DMA((2,)),
            pltpu.SemaphoreType.DMA((11,)),
            pltpu.SemaphoreType.DMA((11,)),
            pltpu.SemaphoreType.DMA((2,)),
            pltpu.SemaphoreType.DMA((2,)),
        ]
        hbm = pl.BlockSpec(memory_space=pl.ANY)
        vmem = pl.BlockSpec(memory_space=pltpu.VMEM)
        smem = pl.BlockSpec(memory_space=pltpu.SMEM)
        return pl.pallas_call(
            functools.partial(kernel, n_head, tokens),
            out_shape=(
                jax.ShapeDtypeStruct(whole, F32),
                jax.ShapeDtypeStruct((batch, 1, DH, DH), F32),
            ),
            in_specs=[hbm, hbm, hbm, hbm, vmem, smem, smem, vmem],
            out_specs=(hbm, vmem),
            scratch_shapes=scratch,
            compiler_params=pltpu.CompilerParams(
                collective_id=0, has_side_effects=True, vmem_limit_bytes=50 * 2**20
            ),
            cost_estimate=pl.CostEstimate(
                flops=2 * 10**10, bytes_accessed=12 * 2**20, transcendentals=0
            ),
        )(
            query_rows, key_rows, value_rows, cotangent, selector, level_table, span_length,
            norm_gain.reshape(1, DH),
        )

    return jax.shard_map(
        local,
        mesh=mesh,
        in_specs=(
            P(None, "seq", "head"),
            P(None, "seq", "head"),
            P(None, "seq", "head"),
            P(None, "seq", "head"),
            P(None, "head", "seq"),
            P(),
            P(None, "seq"),
            P("head"),
        ),
        out_specs=(P(None, "seq", "head"), P(None, "seq", None, "head")),
        check_vma=False,
    )
```

time: 167 us -> 58.6 us (0.35)
  matrix products: 86 us -> 0 us
  Pallas kernels: 0 us -> 52.9 us
  blocking collectives: 33.6 us -> 0 us
  starting transfers between devices: 14.7 us -> 0 us
  waiting for transfers between devices: 12 us -> 0 us
  other arithmetic: 11 us -> 0 us
  local copies, waits for them, and re-layouts: 8.07 us -> 4.85 us
    dot_general x10 -> x0, matrix products: 86 us -> none  [the longest x1 31.8 us: local(): jnp.einsum('bthd,bshd->bhts', queries, live_keys, precision=highest)]
    pallas_call x0 -> x1, Pallas kernels: none -> 52.9 us  [local(): pl.pallas_call(functools.partial(kernel, n_head, tokens), out_shape=(jax....]
    all_to_all x1 -> x0, blocking collectives: 33.6 us -> none  [copy_for_each(): return lax.all_to_all(copies, axis, split_axis=0, concat_axis=0, tiled=True)]
    ppermute x6 -> x0, starting transfers between devices: 14.7 us -> none  [partner(): lax.ppermute(shard, axis, [(i, i ^ 1 << stride) for i in range(lax.axis_s...]
    ppermute x6 -> x0, waiting for transfers between devices: 12 us -> none  [partner(): lax.ppermute(shard, axis, [(i, i ^ 1 << stride) for i in range(lax.axis_s...]
    sub x1 -> x0, other arithmetic: 4.31 us -> none  [local(): scaled * inverse[..., None]]
    le x1 -> x0, other arithmetic: 4.19 us -> none  [local(): causal = position[None, :] <= position[:, None]]
    unnamed x25 -> x8, local copies, waits for them, and re-layouts: 7.11 us -> 4.85 us
  transfers between devices with their start and end apart: 6 -> 0, of which waited for: 4 -> 0; matrix products, arithmetic and copies ran while one was open for 43% -> 0% of each run, Pallas kernels for 0% -> 0%
where the time goes in v1:
time: 58.6 us; the launch traced here: 58.4 us
  Pallas kernels  52.9 us (90%)
  local copies, waits for them, and re-layouts  4.85 us (8%)
  between operations  0.64 us (1%)
    pallas_call x1, Pallas kernels, local(): pl.pallas_call(functools.partial(kernel, n_head, tokens), out_shape=(jax....  52.9 us
    unnamed x8, local copies, waits for them, and re-layouts  4.85 us

profile of v1, /device:TPU:1, one launch (start us, length us, event | category | flops | bytes accessed | tf_op | source)
XLA Modules:
  0.0 58.4 jit_solution(10369899848795881879)
XLA Ops:
  0.6 0.7 %copy.11.span_ref = s32[2,1]{1,0:T(2,128)S(1)} copy(s32[2,1]{0,1:T(1,128)} %param.14) | data formatting | bytes 16 | tf_op args[6]
  1.4 0.8 %copy.10.tab_ref = f32[16,4]{1,0:T(8,128)S(1)} copy(f32[16,4]{0,1:T(4,128)} %param.13) | data formatting | bytes 512 | tf_op args[5]
  2.1 0.0 copy-start
  2.1 0.7 %copy-done = s32[2,1,2048]{2,1,0:T(1,128)S(1)} copy-done((s32[2,1,2048]{2,1,0:T(1,128)S(1)}, s32[2,1,2048]{2,1,0:T(1,128)}, u32[]{:S(2)}) %copy-start) | copy-done | bytes 16408
  2.8 0.0 copy-start.1
  2.8 0.7 %copy-done.1 = f32[128]{0:T(128)S(1)} copy-done((f32[128]{0:T(128)S(1)}, f32[128]{0:T(128)}, u32[]{:S(2)}) %copy-start.1) | copy-done | bytes 536
  3.5 52.9 %shard_map.95 = (f32[2,2048,128]{2,1,0:T(8,128)S(1)}, f32[2,1,128,128]{3,2,1,0:T(8,128)S(1)}) custom-call(f32[2,2048,128]{2,1,0:T(8,128)} %q_hbm.1, f32[2,2048,128]{2,1,0:T(8,128)} %k_hbm.1, f32[2,2048,128]{2,1,0:T(8,128)} %v_hbm.1, f32[2,2048,128]{2,1,0:T(8,128)} %c_hbm.1, s32[2,1,2048]{2,1,0:T(1,128)S(1)} %copy-done, f32[16,4]{1,0:T(8,128)S(1)} %copy.10.tab_ref, ...), custom_call_target="tpu_custom_call" | custom-call | flops 20000000000 | bytes 12582912 | tf_op jit(solution)/shard_map/pallas_call | solution.py:352
  56.4 1.3 %copy.14 = f32[2,2048,128]{2,1,0:T(8,128)} copy(f32[2,2048,128]{2,1,0:T(8,128)S(1)} %get-tuple-element.4) | data formatting | bytes 4194304
  57.8 0.7 %copy.15 = f32[2,1,128,128]{3,2,1,0:T(8,128)} copy(f32[2,1,128,128]{3,2,1,0:T(8,128)S(1)} %get-tuple-element.5) | data formatting | bytes 262144
Async XLA Ops:
  2.1 0.7 %copy-start = (s32[2,1,2048]{2,1,0:T(1,128)S(1)}, s32[2,1,2048]{2,1,0:T(1,128)}, u32[]{:S(2)}) copy-start(s32[2,1,2048]{2,1,0:T(1,128)} %sel_ref.1) | copy-start | bytes 49156
  2.8 0.7 %copy-start.1 = (f32[128]{0:T(128)S(1)}, f32[128]{0:T(128)}, u32[]{:S(2)}) copy-start(f32[128]{0:T(128)} %param.15) | copy-start | bytes 1540

commit v2 on v1

v2 whole, which is shorter than its diff:
```python
import functools

import jax
import jax.numpy as jnp
from jax import lax
from jax.experimental import pallas as pl
from jax.experimental.pallas import tpu as pltpu
from jax.sharding import PartitionSpec as P

DH = 128
CHUNK = 256
WIDE = 2048
U_STATE = 8
U_LOCAL = 4
U_READ = 8
U_ATT = 8
N_X = 4
EPS = 1e-06
F32 = jnp.float32
BF16 = jnp.bfloat16


def split(x):
    high = x.astype(BF16)
    return high, (x - high.astype(F32)).astype(BF16)


def mm(a, b):
    return jnp.dot(a, b, preferred_element_type=F32)


def mm_nt(a, b):
    return lax.dot_general(a, b, (((1,), (1,)), ((), ())), preferred_element_type=F32)


def remote(src, dst, send_sem, recv_sem, device):
    return pltpu.make_async_remote_copy(
        src_ref=src,
        dst_ref=dst,
        send_sem=send_sem,
        recv_sem=recv_sem,
        device_id=device,
        device_id_type=pl.DeviceIdType.MESH,
    )


def kernel(
    n_x, n_z, tokens,
    q_hbm, k_hbm, v_hbm, c_hbm, sel_hbm, tab_hbm, span_hbm, gain_hbm,
    att_ref, sg_ref,
    sel_ref, tab_ref, span_ref, gain_ref,
    qb, kb, vb, cb, kh, kl, vt, pp, wrow, wq, comb, sc, gacc,
    st, b0, pair, b12, far_in, lb, x_in, z_in, coef, gr0, grh, t0, t1, r12, r_in, total,
    load_sem, small_sem, send_sem, recv_sem, h_send, h_recv,
):
    n_chunks = tokens // CHUNK
    half = DH // 2
    seq = lax.axis_index("seq")
    head = lax.axis_index("head")
    core = lax.rem(seq, 2)
    other = 1 - core
    chip = lax.div(seq, 2)
    mate = seq + 1 - 2 * core
    near = 2 * (chip + 1 - 2 * lax.rem(chip, 2)) + core
    far = 2 * (3 - chip) + core
    across = lax.rem(seq + 4, 8)
    x = lax.div(head, n_z)
    z = lax.rem(head, n_z)
    x_peers = [n_z * lax.rem(x + r, n_x) + z for r in range(1, n_x)]
    z_peers = [n_z * x + lax.rem(z + r, n_z) for r in range(1, n_z)]

    def to(peer):
        return {"seq": peer, "head": head}

    def along(peer):
        return {"seq": seq, "head": peer}

    peers = [to(p) for p in (mate, near, far, across)] + [along(p) for p in x_peers + z_peers]

    small = [
        pltpu.make_async_copy(src, dst, small_sem.at[i])
        for i, (src, dst) in enumerate(
            ((tab_hbm, tab_ref), (span_hbm, span_ref), (sel_hbm, sel_ref), (gain_hbm, gain_ref))
        )
    ]
    for copy in small:
        copy.start()
    loads = {}
    pairs = (("k", k_hbm, kb), ("v", v_hbm, vb), ("q", q_hbm, qb), ("c", c_hbm, cb))
    for first in (0, 2):
        for b in range(2):
            for i in (first, first + 1):
                name, src, dst = pairs[i]
                loads[name, b] = pltpu.make_async_copy(src.at[b], dst.at[b], load_sem.at[i, b])
                loads[name, b].start()

    barrier = pltpu.get_barrier_semaphore()
    for peer in peers:
        pl.semaphore_signal(barrier, 1, device_id=peer, device_id_type=pl.DeviceIdType.MESH)

    for copy in small:
        copy.wait()
    selector = [sel_ref[b] for b in range(2)]
    for level in range(4):
        on = 1 if level == 0 else lax.rem(lax.div(seq, 2 ** (level - 1)), 2)
        for b in range(2):
            row = jnp.zeros((1, tokens), F32)
            for choice in range(16):
                row = jnp.where(selector[b] == choice, tab_ref[level, choice], row)
            if level > 0:
                row = jnp.where(on == 1, row, 0.0)
            wrow[level * 2 + b] = row

    def lanes(n):
        return pl.ds(pl.multiple_of(n * CHUNK, CHUNK), CHUNK)

    def states(b):
        span = span_ref[0, b]

        def step(i, acc):
            for u in range(U_STATE):
                n = i * U_STATE + u
                rows = lanes(n)
                position = n * CHUNK + lax.broadcasted_iota(jnp.int32, (CHUNK, DH), 0)
                k_hi, k_lo = split(jnp.where(position < span, kb[b, rows, :], 0.0))
                kh[b, rows, :] = k_hi
                kl[b, rows, :] = k_lo
                v_hi, v_lo = split(vb[b, rows, :].T)
                v_two = jnp.concatenate([v_hi, v_lo], axis=0)
                vt[b, n] = v_two
                p_hi, p_lo = split(acc)
                pp[b, n] = jnp.concatenate([p_hi, p_lo], axis=0)
                out = mm(v_two, jnp.concatenate([k_hi, k_lo], axis=1))
                acc = acc + (out[:DH, :DH] + (out[:DH, DH:] + out[DH:, :DH]))
            return acc

        st[b] = lax.fori_loop(0, n_chunks // U_STATE, step, jnp.zeros((DH, DH), F32))

    def local_chunk(b, n):
        rows = lanes(n)
        q_t = qb[b, rows, :].T
        q_hi, q_lo = split(q_t)
        k_hi, k_lo = kh[b, rows, :], kl[b, rows, :]
        scores = mm(
            jnp.concatenate([k_hi, k_hi, k_lo], axis=1), jnp.concatenate([q_hi, q_lo, q_hi], axis=0)
        )
        key_at = lax.broadcasted_iota(jnp.int32, (CHUNK, CHUNK), 0)
        query_at = lax.broadcasted_iota(jnp.int32, (CHUNK, CHUNK), 1)
        s_hi, s_lo = split(jnp.where(key_at <= query_at, scores, 0.0))
        v_two, p_two = vt[b, n], pp[b, n]
        out = mm(
            jnp.concatenate([v_two, v_two, p_two, p_two], axis=1),
            jnp.concatenate([s_hi, s_lo, q_hi, q_lo], axis=0),
        )
        comb[b, n] = (out[:DH] + out[DH:]) * wrow[b, :, rows]
        for level in range(3):
            w_hi, w_lo = split(q_t * wrow[2 * (level + 1) + b, :, rows])
            wq[b, level * DH : (level + 1) * DH, rows] = w_hi
            wq[b, (3 + level) * DH : (4 + level) * DH, rows] = w_lo
        sc[b, n] = (cb[b, rows, :] * gain_ref[...]).T

    def local_chunks(b, low, high):
        @pl.loop(0, (high - low) // U_LOCAL)
        def _(i):
            for u in range(U_LOCAL):
                local_chunk(b, low + i * U_LOCAL + u)

    for b in range(2):
        loads["k", b].wait()
        loads["v", b].wait()
        states(b)

    pl.semaphore_wait(barrier, len(peers))

    s1, s2, s4 = {}, {}, {}
    for b in range(2):
        s1[b] = remote(st.at[b], b0.at[b], send_sem.at[0, b], recv_sem.at[0, b], to(mate))
        s1[b].start()

    def sum_pair(b):
        s1[b].wait_recv()
        mine = pl.ds(pl.multiple_of(core * half, half), half)
        pair[b] = st[b, mine, :] + b0[b, mine, :]
        s2[b] = [
            remote(pair.at[b], far_in.at[b, 0], send_sem.at[1, b], recv_sem.at[1, b], to(across)),
            remote(pair.at[b], far_in.at[b, 1], send_sem.at[2, b], recv_sem.at[2, b], to(far)),
            remote(pair.at[b], b12.at[b, core, 0], send_sem.at[3, b], recv_sem.at[3, b], to(near)),
        ]
        for copy in s2[b]:
            copy.start()

    def sum_quad(b):
        for copy in s2[b]:
            copy.wait_recv()
        b12[b, core, 1] = far_in[b, 0] + far_in[b, 1]
        s4[b] = remote(
            b12.at[b, core], b12.at[b, core], send_sem.at[4, b], recv_sem.at[4, b], to(mate)
        )
        s4[b].start()

    middle = n_chunks // 2
    loads["q", 0].wait()
    loads["c", 0].wait()
    local_chunks(0, 0, middle)
    sum_pair(0)
    sum_pair(1)
    local_chunks(0, middle, n_chunks)
    loads["q", 1].wait()
    loads["c", 1].wait()
    local_chunks(1, 0, middle)
    sum_quad(0)
    sum_quad(1)
    local_chunks(1, middle, n_chunks)

    def reads(b):
        halves = [split(b0[b])]
        for level in range(2):
            halves.append(split(jnp.concatenate([b12[b, 0, level], b12[b, 1, level]], axis=0)))
        high = jnp.concatenate([h[0] for h in halves], axis=1)
        low = jnp.concatenate([h[1] for h in halves], axis=1)
        lb[b, :DH] = jnp.concatenate([high, high], axis=1)
        lb[b, DH:] = jnp.concatenate([low, low], axis=1)

        @pl.loop(0, n_chunks // U_READ)
        def _(i):
            for u in range(U_READ):
                n = i * U_READ + u
                out = mm(lb[b], wq[b, :, lanes(n)])
                mixed = comb[b, n] + (out[:DH] + out[DH:])
                comb[b, n] = mixed
                x_in[b, x, pl.ds(n, 1), :] = jnp.sum(mixed * mixed, axis=0, keepdims=True)
                x_in[b, x, pl.ds(n_chunks + n, 1), :] = jnp.sum(
                    sc[b, n] * mixed, axis=0, keepdims=True
                )

    def send_x(b):
        for peer in reversed(x_peers):
            remote(x_in.at[b, x], x_in.at[b, x], h_send.at[0, b], h_recv.at[0, b], along(peer)).start()

    def arrived(buffer, count, sem):
        window = buffer.at[pl.ds(0, count)]
        pltpu.make_async_copy(window, window, sem).wait()

    def send_z(b):
        arrived(x_in.at[b], n_x - 1, h_recv.at[0, b])
        z_in[b, z] = jnp.sum(x_in[b], axis=0)
        for peer in sorted(range(1, n_z), key=lambda r: -min(r, n_z - r)):
            remote(
                z_in.at[b, z], z_in.at[b, z], h_send.at[1, b], h_recv.at[1, b],
                along(z_peers[peer - 1]),
            ).start()

    def coefficients(b):
        arrived(z_in.at[b], n_z - 1, h_recv.at[1, b])
        whole = jnp.sum(z_in[b], axis=0)
        width = n_x * n_z * DH
        inverse = lax.rsqrt(whole[:n_chunks] / width + EPS)
        coef[b, :n_chunks] = inverse
        coef[b, n_chunks:] = inverse * inverse * inverse * whole[n_chunks:] / width

    for b in range(2):
        s4[b].wait_recv()
        reads(b)
        send_x(b)
    for b in range(2):
        send_z(b)

    def level_grads(b):
        gacc[...] = jnp.zeros_like(gacc)
        pieces = WIDE // CHUNK

        @pl.loop(0, tokens // WIDE)
        def _(n):
            parts = []
            for i in range(pieces):
                m = n * pieces + i
                grad = sc[b, m] * coef[b, pl.ds(m, 1), :] - comb[b, m] * coef[b, pl.ds(n_chunks + m, 1), :]
                parts.append(jnp.concatenate(split(grad), axis=0))
            rows = pl.ds(pl.multiple_of(n * WIDE, WIDE), WIDE)
            gacc[...] += mm_nt(wq[b, :, rows], jnp.concatenate(parts, axis=1))

        for level in range(3):
            top = slice(level * DH, (level + 1) * DH)
            bottom = slice((3 + level) * DH, (4 + level) * DH)
            grad = gacc[top, :DH] + (gacc[top, DH:] + gacc[bottom, :DH])
            if level == 0:
                gr0[b] = grad
            else:
                grh[b, 0, level - 1] = grad[:half]
                grh[b, 1, level - 1] = grad[half:]

    def attended(b):
        @pl.loop(0, n_chunks // U_ATT)
        def _(i):
            for u in range(U_ATT):
                n = i * U_ATT + u
                att_ref[b, lanes(n), :] = (comb[b, n] * coef[b, pl.ds(n, 1), :]).T * gain_ref[...]

    g1, g2, g4 = {}, {}, {}

    def send_mate(b):
        g1[b] = [
            remote(grh.at[b, other], t1.at[b], send_sem.at[5, b], recv_sem.at[5, b], to(mate)),
            remote(gr0.at[b], t0.at[b], send_sem.at[6, b], recv_sem.at[6, b], to(mate)),
        ]
        for copy in g1[b]:
            copy.start()

    def send_chips(b):
        g1[b][0].wait_recv()
        r12[b] = grh[b, core] + t1[b]
        g2[b] = [
            remote(r12.at[b, 1], r_in.at[b, 0], send_sem.at[7, b], recv_sem.at[7, b], to(across)),
            remote(r12.at[b, 1], r_in.at[b, 1], send_sem.at[8, b], recv_sem.at[8, b], to(far)),
            remote(r12.at[b, 0], r_in.at[b, 2], send_sem.at[9, b], recv_sem.at[9, b], to(near)),
        ]
        for copy in g2[b]:
            copy.start()

    def send_total(b):
        for copy in g2[b]:
            copy.wait_recv()
        total[b, core] = r_in[b, 0] + r_in[b, 1] + r_in[b, 2]
        g4[b] = remote(
            total.at[b, core], total.at[b, core], send_sem.at[10, b], recv_sem.at[10, b], to(mate)
        )
        g4[b].start()

    for b in range(2):
        coefficients(b)
        level_grads(b)
        send_mate(b)
    send_chips(0)
    send_chips(1)
    attended(0)
    attended(1)
    send_total(0)
    send_total(1)
    for b in range(2):
        g1[b][1].wait_recv()
        g4[b].wait_recv()
        sg_ref[b, 0, :half] = total[b, 0] + t0[b, :half]
        sg_ref[b, 0, half:] = total[b, 1] + t0[b, half:]

    for b in range(2):
        for copy in (s1[b], s4[b], g4[b], *s2[b], *g1[b], *g2[b]):
            copy.wait_send()
        arrived(x_in.at[b], n_x - 1, h_send.at[0, b])
        arrived(z_in.at[b], n_z - 1, h_send.at[1, b])


def solution(mesh):
    n_z = mesh.shape["head"] // N_X

    def local(
        query_rows, key_rows, value_rows, cotangent, selector, level_table, span_length, norm_gain
    ):
        batch, tokens, _ = query_rows.shape
        n_chunks = tokens // CHUNK
        square = (DH, DH)
        half = (DH // 2, DH)
        whole = (batch, tokens, DH)
        scratch = [
            pltpu.VMEM((batch, 1, tokens), jnp.int32),
            pltpu.SMEM((4, 16), F32),
            pltpu.SMEM((1, batch), jnp.int32),
            pltpu.VMEM((1, DH), F32),
        ]
        scratch += [pltpu.VMEM(whole, F32) for _ in range(4)]
        scratch += [
            pltpu.VMEM(whole, BF16),
            pltpu.VMEM(whole, BF16),
            pltpu.VMEM((batch, n_chunks, 2 * DH, CHUNK), BF16),
            pltpu.VMEM((batch, n_chunks, 2 * DH, DH), BF16),
            pltpu.VMEM((4 * batch, 1, tokens), F32),
            pltpu.VMEM((batch, 6 * DH, tokens), BF16),
            pltpu.VMEM((batch, n_chunks, DH, CHUNK), F32),
            pltpu.VMEM((batch, n_chunks, DH, CHUNK), F32),
            pltpu.VMEM((6 * DH, 2 * DH), F32),
            pltpu.VMEM((batch, *square), F32),
            pltpu.VMEM((batch, *square), F32),
            pltpu.VMEM((batch, *half), F32),
            pltpu.VMEM((batch, 2, 2, *half), F32),
            pltpu.VMEM((batch, 2, *half), F32),
            pltpu.VMEM((batch, 2 * DH, 6 * DH), BF16),
            pltpu.VMEM((batch, N_X, 2 * n_chunks, CHUNK), F32),
            pltpu.VMEM((batch, n_z, 2 * n_chunks, CHUNK), F32),
            pltpu.VMEM((batch, 2 * n_chunks, CHUNK), F32),
            pltpu.VMEM((batch, *square), F32),
            pltpu.VMEM((batch, 2, 2, *half), F32),
            pltpu.VMEM((batch, *square), F32),
            pltpu.VMEM((batch, 2, *half), F32),
            pltpu.VMEM((batch, 2, *half), F32),
            pltpu.VMEM((batch, 3, *half), F32),
            pltpu.VMEM((batch, 2, *half), F32),
            pltpu.SemaphoreType.DMA((4, 2)),
            pltpu.SemaphoreType.DMA((4,)),
            pltpu.SemaphoreType.DMA((11, 2)),
            pltpu.SemaphoreType.DMA((11, 2)),
            pltpu.SemaphoreType.DMA((2, 2)),
            pltpu.SemaphoreType.DMA((2, 2)),
        ]
        hbm = pl.BlockSpec(memory_space=pltpu.HBM)
        vmem = pl.BlockSpec(memory_space=pltpu.VMEM)
        return pl.pallas_call(
            functools.partial(kernel, N_X, n_z, tokens),
            out_shape=(
                jax.ShapeDtypeStruct(whole, F32),
                jax.ShapeDtypeStruct((batch, 1, DH, DH), F32),
            ),
            in_specs=[hbm] * 8,
            out_specs=(vmem, vmem),
            scratch_shapes=scratch,
            compiler_params=pltpu.CompilerParams(
                collective_id=0, has_side_effects=True, vmem_limit_bytes=50 * 2**20
            ),
            cost_estimate=pl.CostEstimate(
                flops=2 * 10**10, bytes_accessed=12 * 2**20, transcendentals=0
            ),
        )(
            query_rows, key_rows, value_rows, cotangent,
            *(
                pltpu.with_memory_space_constraint(small, pltpu.HBM)
                for small in (selector, level_table.T, span_length.T, norm_gain.reshape(1, DH))
            ),
        )

    return jax.shard_map(
        local,
        mesh=mesh,
        in_specs=(
            P(None, "seq", "head"),
            P(None, "seq", "head"),
            P(None, "seq", "head"),
            P(None, "seq", "head"),
            P(None, "head", "seq"),
            P(),
            P(None, "seq"),
            P("head"),
        ),
        out_specs=(P(None, "seq", "head"), P(None, "seq", None, "head")),
        check_vma=False,
    )
```

time: 58.6 us -> 42.6 us (0.73)
  Pallas kernels: 52.9 us -> 39.9 us
  local copies, waits for them, and re-layouts: 4.85 us -> 1.98 us
    pallas_call x1, Pallas kernels: 52.9 us -> 39.9 us  [local(): pl.pallas_call(functools.partial(kernel, N_X, n_z, tokens), out_shape=(ja...]
    unnamed x8 -> x2, local copies, waits for them, and re-layouts: 4.85 us -> 1.98 us
where the time goes in v2:
time: 42.6 us; the launch traced here: 42.5 us
  Pallas kernels  39.9 us (94%)
  local copies, waits for them, and re-layouts  1.98 us (5%)
  between operations  0.64 us (2%)
    pallas_call x1, Pallas kernels, local(): pl.pallas_call(functools.partial(kernel, N_X, n_z, tokens), out_shape=(ja...  39.9 us
    unnamed x2, local copies, waits for them, and re-layouts  1.98 us

profile of v2, /device:TPU:1, one launch (start us, length us, event | category | flops | bytes accessed | tf_op | source)
XLA Modules:
  0.0 42.5 jit_solution(2357580901666822887)
XLA Ops:
  0.6 39.9 %shard_map.95 = (f32[2,2048,128]{2,1,0:T(8,128)S(1)}, f32[2,1,128,128]{3,2,1,0:T(8,128)S(1)}) custom-call(f32[2,2048,128]{2,1,0:T(8,128)} %q_hbm.1, f32[2,2048,128]{2,1,0:T(8,128)} %k_hbm.1, f32[2,2048,128]{2,1,0:T(8,128)} %v_hbm.1, f32[2,2048,128]{2,1,0:T(8,128)} %c_hbm.1, s32[2,1,2048]{2,1,0:T(1,128)} %sel_hbm.1, f32[4,16]{1,0:T(4,128)} %bitcast.3, ...), custom_call_target="tpu_custom_call" | custom-call | flops 20000000000 | bytes 12582912 | tf_op jit(solution)/shard_map/pallas_call | solution.py:405
  40.6 1.3 %copy.12 = f32[2,2048,128]{2,1,0:T(8,128)} copy(f32[2,2048,128]{2,1,0:T(8,128)S(1)} %get-tuple-element.4) | data formatting | bytes 4194304
  41.9 0.7 %copy.13 = f32[2,1,128,128]{3,2,1,0:T(8,128)} copy(f32[2,1,128,128]{3,2,1,0:T(8,128)S(1)} %get-tuple-element.5) | data formatting | bytes 262144

commit v3 on v2

--- a/solution.py
+++ b/solution.py
@@ -9,7 +9,7 @@
 
 DH = 128
 CHUNK = 256
-WIDE = 2048
+WIDE = 1024
 U_STATE = 8
 U_LOCAL = 4
 U_READ = 8
@@ -92,7 +92,13 @@
             for i in (first, first + 1):
                 name, src, dst = pairs[i]
                 loads[name, b] = pltpu.make_async_copy(src.at[b], dst.at[b], load_sem.at[i, b])
-                loads[name, b].start()
+
+    def load(names, b):
+        for name in names:
+            loads[name, b].start()
+
+    load("kv", 0)
+    load("kv", 1)
 
     barrier = pltpu.get_barrier_semaphore()
     for peer in peers:
@@ -165,15 +171,14 @@
             for u in range(U_LOCAL):
                 local_chunk(b, low + i * U_LOCAL + u)
 
+    s1, s2, s4 = {}, {}, {}
     for b in range(2):
         loads["k", b].wait()
         loads["v", b].wait()
+        load("qc", b)
         states(b)
-
-    pl.semaphore_wait(barrier, len(peers))
-
-    s1, s2, s4 = {}, {}, {}
-    for b in range(2):
+        if b == 0:
+            pl.semaphore_wait(barrier, len(peers))
         s1[b] = remote(st.at[b], b0.at[b], send_sem.at[0, b], recv_sem.at[0, b], to(mate))
         s1[b].start()
 
@@ -199,20 +204,19 @@
         s4[b].start()
 
     middle = n_chunks // 2
+    sum_pair(0)
     loads["q", 0].wait()
     loads["c", 0].wait()
     local_chunks(0, 0, middle)
-    sum_pair(0)
     sum_pair(1)
     local_chunks(0, middle, n_chunks)
     loads["q", 1].wait()
     loads["c", 1].wait()
     local_chunks(1, 0, middle)
     sum_quad(0)
-    sum_quad(1)
     local_chunks(1, middle, n_chunks)
 
-    def reads(b):
+    def reads(b, sums):
         halves = [split(b0[b])]
         for level in range(2):
             halves.append(split(jnp.concatenate([b12[b, 0, level], b12[b, 1, level]], axis=0)))
@@ -228,31 +232,39 @@
                 out = mm(lb[b], wq[b, :, lanes(n)])
                 mixed = comb[b, n] + (out[:DH] + out[DH:])
                 comb[b, n] = mixed
-                x_in[b, x, pl.ds(n, 1), :] = jnp.sum(mixed * mixed, axis=0, keepdims=True)
-                x_in[b, x, pl.ds(n_chunks + n, 1), :] = jnp.sum(
-                    sc[b, n] * mixed, axis=0, keepdims=True
-                )
-
-    def send_x(b):
-        for peer in reversed(x_peers):
-            remote(x_in.at[b, x], x_in.at[b, x], h_send.at[0, b], h_recv.at[0, b], along(peer)).start()
+                sums[pl.ds(n, 1), :] = jnp.sum(mixed * mixed, axis=0, keepdims=True)
+                sums[pl.ds(n_chunks + n, 1), :] = jnp.sum(sc[b, n] * mixed, axis=0, keepdims=True)
 
     def arrived(buffer, count, sem):
         window = buffer.at[pl.ds(0, count)]
         pltpu.make_async_copy(window, window, sem).wait()
 
-    def send_z(b):
-        arrived(x_in.at[b], n_x - 1, h_recv.at[0, b])
-        z_in[b, z] = jnp.sum(x_in[b], axis=0)
-        for peer in sorted(range(1, n_z), key=lambda r: -min(r, n_z - r)):
+    z_order = sorted(range(1, n_z), key=lambda r: -min(r, n_z - r))
+    x_stage = (x_in, x, [x_peers[r] for r in (1, 0, 2)], n_x - 1)
+    z_stage = (z_in, z, [z_peers[r - 1] for r in z_order], n_z - 1)
+    stages = ((x_stage, z_stage), (z_stage, x_stage))
+
+    def send_sums(b, step):
+        buffer, mine, others, _ = stages[b][step]
+        for peer in others:
             remote(
-                z_in.at[b, z], z_in.at[b, z], h_send.at[1, b], h_recv.at[1, b],
-                along(z_peers[peer - 1]),
+                buffer.at[b, mine], buffer.at[b, mine], h_send.at[step, b], h_recv.at[step, b],
+                along(peer),
             ).start()
 
+    def receive_sums(b, step):
+        buffer, _, _, count = stages[b][step]
+        arrived(buffer.at[b], count, h_recv.at[step, b])
+        return jnp.sum(buffer[b], axis=0)
+
+    def pass_on(b):
+        partial = receive_sums(b, 0)
+        buffer, mine, _, _ = stages[b][1]
+        buffer[b, mine] = partial
+        send_sums(b, 1)
+
     def coefficients(b):
-        arrived(z_in.at[b], n_z - 1, h_recv.at[1, b])
-        whole = jnp.sum(z_in[b], axis=0)
+        whole = receive_sums(b, 1)
         width = n_x * n_z * DH
         inverse = lax.rsqrt(whole[:n_chunks] / width + EPS)
         coef[b, :n_chunks] = inverse
@@ -260,10 +272,13 @@
 
     for b in range(2):
         s4[b].wait_recv()
-        reads(b)
-        send_x(b)
-    for b in range(2):
-        send_z(b)
+        buffer, mine, _, _ = stages[b][0]
+        reads(b, buffer.at[b, mine])
+        send_sums(b, 0)
+        if b == 0:
+            sum_quad(1)
+    pass_on(0)
+    pass_on(1)
 
     def level_grads(b):
         gacc[...] = jnp.zeros_like(gacc)
@@ -330,10 +345,8 @@
         coefficients(b)
         level_grads(b)
         send_mate(b)
-    send_chips(0)
-    send_chips(1)
-    attended(0)
-    attended(1)
+        attended(b)
+        send_chips(b)
     send_total(0)
     send_total(1)
     for b in range(2):
@@ -345,8 +358,9 @@
     for b in range(2):
         for copy in (s1[b], s4[b], g4[b], *s2[b], *g1[b], *g2[b]):
             copy.wait_send()
-        arrived(x_in.at[b], n_x - 1, h_send.at[0, b])
-        arrived(z_in.at[b], n_z - 1, h_send.at[1, b])
+        for step in range(2):
+            buffer, _, _, count = stages[b][step]
+            arrived(buffer.at[b], count, h_send.at[step, b])
 
 
 def solution(mesh):

time: 42.6 us -> 41 us (0.962)
  Pallas kernels: 39.9 us -> 38.3 us
    pallas_call x1, Pallas kernels: 39.9 us -> 38.3 us  [local(): pl.pallas_call(functools.partial(kernel, N_X, n_z, tokens), out_shape=(ja...]
where the time goes in v3:
time: 41 us; the launch traced here: 40.9 us
  Pallas kernels  38.3 us (93%)
  local copies, waits for them, and re-layouts  1.98 us (5%)
  between operations  0.64 us (2%)
    pallas_call x1, Pallas kernels, local(): pl.pallas_call(functools.partial(kernel, N_X, n_z, tokens), out_shape=(ja...  38.3 us
    unnamed x2, local copies, waits for them, and re-layouts  1.98 us

profile of v3, /device:TPU:1, one launch (start us, length us, event | category | flops | bytes accessed | tf_op | source)
XLA Modules:
  0.0 40.9 jit_solution(14628647904720413506)
XLA Ops:
  0.6 38.3 %shard_map.95 = (f32[2,2048,128]{2,1,0:T(8,128)S(1)}, f32[2,1,128,128]{3,2,1,0:T(8,128)S(1)}) custom-call(f32[2,2048,128]{2,1,0:T(8,128)} %q_hbm.1, f32[2,2048,128]{2,1,0:T(8,128)} %k_hbm.1, f32[2,2048,128]{2,1,0:T(8,128)} %v_hbm.1, f32[2,2048,128]{2,1,0:T(8,128)} %c_hbm.1, s32[2,1,2048]{2,1,0:T(1,128)} %sel_hbm.1, f32[4,16]{1,0:T(4,128)} %bitcast.3, ...), custom_call_target="tpu_custom_call" | custom-call | flops 20000000000 | bytes 12582912 | tf_op jit(solution)/shard_map/pallas_call | solution.py:419
  38.9 1.3 %copy.12 = f32[2,2048,128]{2,1,0:T(8,128)} copy(f32[2,2048,128]{2,1,0:T(8,128)S(1)} %get-tuple-element.4) | data formatting | bytes 4194304
  40.2 0.7 %copy.13 = f32[2,1,128,128]{3,2,1,0:T(8,128)} copy(f32[2,1,128,128]{3,2,1,0:T(8,128)S(1)} %get-tuple-element.5) | data formatting | bytes 262144

commit v4 on v3

--- a/solution.py
+++ b/solution.py
@@ -13,7 +13,7 @@
 U_STATE = 8
 U_LOCAL = 4
 U_READ = 8
-U_ATT = 8
+U_ATT = 4
 N_X = 4
 EPS = 1e-06
 F32 = jnp.float32
@@ -242,7 +242,7 @@
     z_order = sorted(range(1, n_z), key=lambda r: -min(r, n_z - r))
     x_stage = (x_in, x, [x_peers[r] for r in (1, 0, 2)], n_x - 1)
     z_stage = (z_in, z, [z_peers[r - 1] for r in z_order], n_z - 1)
-    stages = ((x_stage, z_stage), (z_stage, x_stage))
+    stages = ((z_stage, x_stage), (x_stage, z_stage))
 
     def send_sums(b, step):
         buffer, mine, others, _ = stages[b][step]

time: 41 us -> 40.3 us (0.983)
  Pallas kernels: 38.3 us -> 37.6 us
    pallas_call x1, Pallas kernels: 38.3 us -> 37.6 us  [local(): pl.pallas_call(functools.partial(kernel, N_X, n_z, tokens), out_shape=(ja...]
where the time goes in v4:
time: 40.3 us; the launch traced here: 40.2 us
  Pallas kernels  37.6 us (93%)
  local copies, waits for them, and re-layouts  1.98 us (5%)
  between operations  0.64 us (2%)
    pallas_call x1, Pallas kernels, local(): pl.pallas_call(functools.partial(kernel, N_X, n_z, tokens), out_shape=(ja...  37.6 us
    unnamed x2, local copies, waits for them, and re-layouts  1.98 us

profile of v4, /device:TPU:1, one launch (start us, length us, event | category | flops | bytes accessed | tf_op | source)
XLA Modules:
  0.0 40.2 jit_solution(7982004351751563690)
XLA Ops:
  0.6 37.6 %shard_map.95 = (f32[2,2048,128]{2,1,0:T(8,128)S(1)}, f32[2,1,128,128]{3,2,1,0:T(8,128)S(1)}) custom-call(f32[2,2048,128]{2,1,0:T(8,128)} %q_hbm.1, f32[2,2048,128]{2,1,0:T(8,128)} %k_hbm.1, f32[2,2048,128]{2,1,0:T(8,128)} %v_hbm.1, f32[2,2048,128]{2,1,0:T(8,128)} %c_hbm.1, s32[2,1,2048]{2,1,0:T(1,128)} %sel_hbm.1, f32[4,16]{1,0:T(4,128)} %bitcast.3, ...), custom_call_target="tpu_custom_call" | custom-call | flops 20000000000 | bytes 12582912 | tf_op jit(solution)/shard_map/pallas_call | solution.py:419
  38.3 1.3 %copy.12 = f32[2,2048,128]{2,1,0:T(8,128)} copy(f32[2,2048,128]{2,1,0:T(8,128)S(1)} %get-tuple-element.4) | data formatting | bytes 4194304
  39.6 0.7 %copy.13 = f32[2,1,128,128]{3,2,1,0:T(8,128)} copy(f32[2,1,128,128]{3,2,1,0:T(8,128)S(1)} %get-tuple-element.5) | data formatting | bytes 262144

commit v5 on v4

--- a/solution.py
+++ b/solution.py
@@ -345,8 +345,9 @@
         coefficients(b)
         level_grads(b)
         send_mate(b)
-        attended(b)
         send_chips(b)
+    attended(0)
+    attended(1)
     send_total(0)
     send_total(1)
     for b in range(2):

time: 40.3 us -> 40.3 us (level)
  no operation moved by 1% of the time
where the time goes in v5:
time: 40.3 us; the launch traced here: 40.2 us
  Pallas kernels  37.6 us (93%)
  local copies, waits for them, and re-layouts  1.98 us (5%)
  between operations  0.64 us (2%)
    pallas_call x1, Pallas kernels, local(): pl.pallas_call(functools.partial(kernel, N_X, n_z, tokens), out_shape=(ja...  37.6 us
    unnamed x2, local copies, waits for them, and re-layouts  1.98 us

profile of v5, /device:TPU:1, one launch (start us, length us, event | category | flops | bytes accessed | tf_op | source)
XLA Modules:
  0.0 40.2 jit_solution(2531195297055205148)
XLA Ops:
  0.6 37.6 %shard_map.95 = (f32[2,2048,128]{2,1,0:T(8,128)S(1)}, f32[2,1,128,128]{3,2,1,0:T(8,128)S(1)}) custom-call(f32[2,2048,128]{2,1,0:T(8,128)} %q_hbm.1, f32[2,2048,128]{2,1,0:T(8,128)} %k_hbm.1, f32[2,2048,128]{2,1,0:T(8,128)} %v_hbm.1, f32[2,2048,128]{2,1,0:T(8,128)} %c_hbm.1, s32[2,1,2048]{2,1,0:T(1,128)} %sel_hbm.1, f32[4,16]{1,0:T(4,128)} %bitcast.3, ...), custom_call_target="tpu_custom_call" | custom-call | flops 20000000000 | bytes 12582912 | tf_op jit(solution)/shard_map/pallas_call | solution.py:420
  38.3 1.3 %copy.12 = f32[2,2048,128]{2,1,0:T(8,128)} copy(f32[2,2048,128]{2,1,0:T(8,128)S(1)} %get-tuple-element.4) | data formatting | bytes 4194304
  39.6 0.7 %copy.13 = f32[2,1,128,128]{3,2,1,0:T(8,128)} copy(f32[2,1,128,128]{3,2,1,0:T(8,128)S(1)} %get-tuple-element.5) | data formatting | bytes 262144
